TPU v7x, 32 devices: a whole 2x2x4 slice. The times are simulated.
32 devices in a mesh: expert: 8 (over z, x), tensor: 4 (over y, core).
Axes of the slice: x: 2, y: 2, z: 4, core: 2. Of those that a mesh axis runs over, the one named last changes fastest.
Arguments:
- tokens: bfloat16 [4096, 1024], P('expert'), may hold values from -6 to 6
- teacher: bfloat16 [4096, 1024], P('expert'), may hold values from -6 to 6
- valid_mask: int32 [4096], P('expert'), may hold values from 0 to 1, as said below
- routes: int32 [4096, 8], P('expert'), may hold values from 0 to 31, all different within a row; in each aligned block of 512 rows (0 to 511, 512 to 1023, ...) at most 192 rows name the same one
- first_gain: float32 [1024], replicated, may hold values from 0.5 to 1.5
- query_weight: bfloat16 [1024, 1024], P(None, 'tensor'), may hold values from -0.75 to 0.75
- key_matrix: bfloat16 [1024, 512], P(None, 'tensor'), may hold values from -0.75 to 0.75
- value_matrix: bfloat16 [1024, 512], P(None, 'tensor'), may hold values from -0.1875 to 0.1875
- output_weight: bfloat16 [1024, 1024], P('tensor'), may hold values from -3 to 3
- second_gain: float32 [1024], replicated, may hold values from 0.5 to 1.5
- router_weight: bfloat16 [1024, 32], replicated, may hold values from -0.09375 to 0.09375
- expert_in: bfloat16 [64, 2, 512, 512], P('expert', None, None, 'tensor'), may hold values from -0.1875 to 0.1875
- expert_out: bfloat16 [64, 512, 512], P('expert', 'tensor'), may hold values from -3 to 3
Outputs:
- layer_output: bfloat16 [4096, 1024], P('expert')
- mean_loss: float32 [], replicated
- grad_tokens: float32 [4096, 1024], P('expert')
- grad_first_gain: float32 [1024], replicated
- grad_query: float32 [1024, 1024], P(None, 'tensor')
- grad_key: float32 [1024, 512], P(None, 'tensor')
- grad_value: float32 [1024, 512], P(None, 'tensor')
- grad_output: float32 [1024, 1024], P('tensor')
- grad_second_gain: float32 [1024], replicated
- grad_router: float32 [1024, 32], replicated
- grad_expert_in: float32 [64, 2, 512, 512], P('expert', None, None, 'tensor')
- grad_expert_out: float32 [64, 512, 512], P('expert', 'tensor')
Inputs may be any that keep to these rules, and one draw needn't show every extreme that they name: `routes`: each row names 8 different experts; among the 512 rows of one device no expert is named more than 192 times, a bound that some block reaches. `valid_mask`: the last of each device's 512 rows is 1.
All inputs are finite; a program needn't handle non-finite values.
Results may differ from a plain program's by a relative error of at most 0.017.
The roundings to bfloat16 on the way count: a program that leaves them out, or rounds other values in their place, can miss the bound.
Values may be sent and summed in bfloat16 or wider, within the bound.
No kernel may reach another device: no remote copies, remote signals or barrier semaphores. Data moves between devices by JAX's collectives and lax.ppermute only.
A program may use at most 192 MiB of HBM per device.

v0:
```python
import jax
import jax.numpy as jnp
from jax import lax
from jax.sharding import PartitionSpec as P

HEAD_DIM = 64
TOP = 8
BLOCK = 256
EPS = 1e-06
ATTN_SCALE = 0.015625
RESIDUAL = 0.22
THETA = 10000.0


def shifted(value, axis, steps):
    count = lax.axis_size(axis)
    pairs = [(source, (source + steps) % count) for source in range(count)]
    return lax.ppermute(value, axis, pairs)


def rope_tables(length, head_size):
    half_size = head_size // 2
    frequency = THETA ** (-(jnp.arange(half_size, dtype=jnp.float32) * 2.0) / head_size)
    angle_table = jnp.arange(length, dtype=jnp.float32)[:, None] * frequency[None, :]
    return (jnp.cos(angle_table)[:, None, :], jnp.sin(angle_table)[:, None, :])


def apply_rotary(values, cosine_lookup, sine_lookup):
    half_size = values.shape[-1] // 2
    lower_half, upper_half = (values[..., :half_size], values[..., half_size:])
    return jnp.concatenate(
        [
            lower_half * cosine_lookup - upper_half * sine_lookup,
            upper_half * cosine_lookup + lower_half * sine_lookup,
        ],
        -1,
    )


def unrotate(grads, cosine_lookup, sine_lookup):
    half_size = grads.shape[-1] // 2
    lower_half, upper_half = (grads[..., :half_size], grads[..., half_size:])
    return jnp.concatenate(
        [
            lower_half * cosine_lookup + upper_half * sine_lookup,
            upper_half * cosine_lookup - lower_half * sine_lookup,
        ],
        -1,
    )


def normalize(values):
    row_peak = jnp.max(values, -1, keepdims=True)
    exp_scores = jnp.exp(values - row_peak)
    return exp_scores / jnp.sum(exp_scores, -1, keepdims=True)


def slot_tables(route_ids, expert_count, capacity):
    row_count, top_count = route_ids.shape
    onehot = route_ids[:, :, None] == jnp.arange(expert_count, dtype=jnp.int32)[None, None, :]
    hit_count = jnp.sum(onehot.astype(jnp.int32), 1)
    slot_place = jnp.cumsum(hit_count, 0) - 1
    within = jnp.take_along_axis(slot_place, route_ids, 1)
    dest_slot = route_ids * capacity + within
    pair_count = row_count * top_count
    source = (
        jnp.full((expert_count * capacity,), pair_count, jnp.int32)
        .at[dest_slot.reshape(-1)]
        .set(jnp.arange(pair_count, dtype=jnp.int32))
    )
    live_slot = source < pair_count
    token_row = jnp.minimum(source, pair_count - 1) // top_count
    return (onehot, dest_slot, source, live_slot, token_row)


def per_device(
    tokens,
    teacher,
    valid_mask,
    routes,
    first_gain,
    query_weight,
    key_matrix,
    value_matrix,
    output_weight,
    second_gain,
    router_weight,
    expert_in,
    expert_out,
):
    row_count = tokens.shape[0]
    model_width = tokens.shape[1]
    half_width = model_width // 2
    local_query = query_weight.shape[1] // HEAD_DIM
    local_kv = key_matrix.shape[1] // HEAD_DIM
    query_group_size = local_query // local_kv
    expert_count = router_weight.shape[1]
    row_local = expert_in.shape[0]
    senders = lax.axis_size("expert")
    partner_step = senders // 2
    capacity = 3 * row_count * TOP // (2 * expert_count)
    pair_count = row_count * TOP
    score_rows = min(512, row_count)
    valid_total = lax.psum(jnp.sum(valid_mask).astype(jnp.float32), "expert")
    tokens_f32 = tokens.astype(jnp.float32)
    scale_one = lax.rsqrt(jnp.mean(tokens_f32 * tokens_f32, -1, keepdims=True) + EPS)
    unit_one = tokens_f32 * scale_one
    first_normed = (unit_one * first_gain).astype(jnp.bfloat16)
    cosine_lookup, sine_lookup = rope_tables(row_count, HEAD_DIM)
    query_linear = jnp.dot(first_normed, query_weight, preferred_element_type=jnp.float32).reshape(
        row_count, local_query, HEAD_DIM
    )
    keys_linear = jnp.dot(first_normed, key_matrix, preferred_element_type=jnp.float32).reshape(
        row_count, local_kv, HEAD_DIM
    )
    value_low = jnp.dot(first_normed, value_matrix, preferred_element_type=jnp.float32).astype(
        jnp.bfloat16
    )
    value_low = value_low.reshape(row_count, local_kv, HEAD_DIM)
    query_rotated = apply_rotary(query_linear, cosine_lookup, sine_lookup).astype(jnp.bfloat16)
    keys_rot = apply_rotary(keys_linear, cosine_lookup, sine_lookup).astype(jnp.bfloat16)
    block_of = jnp.arange(row_count, dtype=jnp.int32) // BLOCK

    def scores(start_row):
        stop_row = start_row + score_rows
        query_block = query_rotated.reshape(score_rows, local_kv, query_group_size, HEAD_DIM)
        score_block = (
            jnp.einsum("qhgd,khd->hgqk", query_block, keys_rot, preferred_element_type=jnp.float32)
            * ATTN_SCALE
        )
        allowed = block_of[None, :stop_row] <= block_of[start_row:stop_row, None]
        return (query_block, jnp.where(allowed, score_block, -1e30))

    attn_parts, row_peaks, row_totals = ([], [], [])
    start_row = 0
    query_block, score_block = scores(start_row)
    row_peak = jnp.max(score_block, -1, keepdims=True)
    exp_scores = jnp.exp(score_block - row_peak)
    row_total = jnp.sum(exp_scores, -1, keepdims=True)
    attn_probs = (exp_scores / row_total).astype(jnp.bfloat16)
    attn_parts.append(
        jnp.einsum("hgqk,khd->qhgd", attn_probs, value_low, preferred_element_type=jnp.float32)
    )
    row_peaks.append(row_peak)
    row_totals.append(row_total)
    attended = attn_parts[0].reshape(row_count, local_query * HEAD_DIM).astype(jnp.bfloat16)
    attn_part = jnp.dot(attended, output_weight, preferred_element_type=jnp.float32)
    attn_sum = lax.psum(attn_part, "tensor")
    hidden_state = tokens_f32 + RESIDUAL * attn_sum
    scale_two = lax.rsqrt(jnp.mean(hidden_state * hidden_state, -1, keepdims=True) + EPS)
    unit_two = hidden_state * scale_two
    normed_two = (unit_two * second_gain).astype(jnp.bfloat16)
    router_logits = jnp.dot(normed_two, router_weight, preferred_element_type=jnp.float32)
    onehot, dest_slot, source, live_slot, token_row = slot_tables(routes, expert_count, capacity)
    picked = jnp.sum(jnp.where(onehot, router_logits[:, None, :], 0.0), -1)
    gate_probs = normalize(picked)

    def slot_rows(slot_values):
        split_rows = slot_values.reshape(expert_count, capacity, 2, half_width).transpose(
            2, 0, 1, 3
        )
        return split_rows.reshape(senders, row_local, capacity, half_width)

    def slot_columns(returned, width):
        joined = returned.reshape(2, expert_count, capacity, width).transpose(1, 2, 0, 3)
        return joined.reshape(expert_count * capacity, 2, width)

    send_rows = slot_rows(
        jnp.where(live_slot[:, None], normed_two[token_row], jnp.zeros((), jnp.bfloat16))
    )
    received = lax.all_to_all(send_rows, "expert", split_axis=0, concat_axis=2, tiled=True)
    expert_rows = received.reshape(row_local, senders * capacity, half_width)
    gate_up_part = jnp.einsum(
        "rmd,rcdf->rmcf", expert_rows, expert_in, preferred_element_type=jnp.float32
    )
    gate_up_pre = gate_up_part + shifted(gate_up_part, "expert", partner_step)
    gate_pre = gate_up_pre[:, :, 0]
    up_pre = gate_up_pre[:, :, 1]
    inner_act = (jax.nn.silu(gate_pre) * up_pre).astype(jnp.bfloat16)
    expert_result = jnp.einsum(
        "rmf,rfd->rmd", inner_act, expert_out, preferred_element_type=jnp.float32
    )
    expert_result = expert_result.astype(jnp.bfloat16).reshape(
        row_local, senders, capacity, half_width
    )
    returned = lax.all_to_all(expert_result, "expert", split_axis=1, concat_axis=0, tiled=True)
    per_route = slot_columns(returned, half_width).reshape(expert_count * capacity, model_width)[
        dest_slot
    ]
    moe_part = jnp.sum(gate_probs[:, :, None] * per_route, 1)
    moe_sum = lax.psum(moe_part, "tensor")
    output = hidden_state + RESIDUAL * moe_sum
    residual_err = output - teacher.astype(jnp.float32)
    valid_rows = valid_mask.astype(jnp.float32)
    squared_local = jnp.sum(valid_rows * jnp.sum(residual_err * residual_err, -1))
    token_total = senders * row_count
    grad_out = token_total / valid_total * valid_rows[:, None] * residual_err
    grad_moe = (RESIDUAL * grad_out).astype(jnp.bfloat16)
    gate_part = jnp.einsum("td,tkd->tk", grad_moe, per_route, preferred_element_type=jnp.float32)
    gate_slot = gate_probs.reshape(pair_count)[jnp.minimum(source, pair_count - 1)]
    grad_slots = jnp.where(live_slot[:, None], gate_slot[:, None] * grad_moe[token_row], 0.0)
    grad_received = lax.all_to_all(
        slot_rows(grad_slots.astype(jnp.bfloat16)),
        "expert",
        split_axis=0,
        concat_axis=2,
        tiled=True,
    )
    grad_expert = grad_received.reshape(row_local, senders * capacity, half_width)
    grad_inner_part = jnp.einsum(
        "rmd,rfd->rmf", grad_expert, expert_out, preferred_element_type=jnp.float32
    )
    grad_inner = grad_inner_part + shifted(grad_inner_part, "expert", partner_step)
    grad_expert_out = jnp.einsum(
        "rmf,rmd->rfd", inner_act, grad_expert, preferred_element_type=jnp.float32
    )
    sigmoid_gate = jax.nn.sigmoid(gate_pre)
    grad_gate = grad_inner * up_pre * sigmoid_gate * (1.0 + gate_pre * (1.0 - sigmoid_gate))
    grad_up = grad_inner * (gate_pre * sigmoid_gate)
    grad_pre = jnp.stack([grad_gate, grad_up], 2).astype(jnp.bfloat16)
    grad_expert_in = jnp.einsum(
        "rmd,rmcf->rcdf", expert_rows, grad_pre, preferred_element_type=jnp.float32
    )
    grad_slot_rows = jnp.einsum(
        "rmcf,rcdf->rmd", grad_pre, expert_in, preferred_element_type=jnp.float32
    )
    grad_slot_rows = grad_slot_rows.astype(jnp.bfloat16).reshape(
        row_local, senders, capacity, half_width
    )
    grad_back = lax.all_to_all(grad_slot_rows, "expert", split_axis=1, concat_axis=0, tiled=True)
    grad_back = slot_columns(grad_back, half_width).reshape(expert_count * capacity, model_width)
    grad_two_part = jnp.sum(grad_back[dest_slot].astype(jnp.float32), 1)
    grad_two_experts, grad_gates = lax.psum((grad_two_part, gate_part), "tensor")
    grad_picked = gate_probs * (grad_gates - jnp.sum(gate_probs * grad_gates, -1, keepdims=True))
    grad_logits = jnp.sum(jnp.where(onehot, grad_picked[:, :, None], 0.0), 1).astype(jnp.bfloat16)
    grad_router = jnp.einsum(
        "td,te->de", normed_two, grad_logits, preferred_element_type=jnp.float32
    )
    grad_two = grad_two_experts + jnp.einsum(
        "te,de->td", grad_logits, router_weight, preferred_element_type=jnp.float32
    )
    grad_second_gain = jnp.sum(grad_two * unit_two, 0)
    grad_unit_two = grad_two * second_gain
    grad_hidden = grad_out + scale_two * (
        grad_unit_two - unit_two * jnp.mean(grad_unit_two * unit_two, -1, keepdims=True)
    )
    grad_attn = (RESIDUAL * grad_hidden).astype(jnp.bfloat16)
    grad_output = jnp.einsum("tc,td->cd", attended, grad_attn, preferred_element_type=jnp.float32)
    grad_attended = jnp.einsum(
        "td,cd->tc", grad_attn, output_weight, preferred_element_type=jnp.float32
    )
    grad_attended = grad_attended.astype(jnp.bfloat16).reshape(
        row_count, local_kv, query_group_size, HEAD_DIM
    )
    grad_query_parts = []
    grad_keys = jnp.zeros((row_count, local_kv, HEAD_DIM), jnp.float32)
    grad_values = jnp.zeros((row_count, local_kv, HEAD_DIM), jnp.float32)
    for block_index, start_row in enumerate(range(0, row_count, score_rows)):
        stop_row = start_row + score_rows
        query_block, score_block = scores(start_row)
        attn_probs = jnp.exp(score_block - row_peaks[block_index]) / row_totals[block_index]
        probs_low = attn_probs.astype(jnp.bfloat16)
        grad_probs = jnp.einsum(
            "qhgd,khd->hgqk", grad_attended, value_low, preferred_element_type=jnp.float32
        )
        grad_scores = attn_probs * (
            grad_probs - jnp.sum(attn_probs * grad_probs, -1, keepdims=True)
        )
        grad_scores = grad_scores.astype(jnp.bfloat16)
        grad_query_parts.append(
            ATTN_SCALE
            * jnp.einsum(
                "hgqk,khd->qhgd", grad_scores, keys_rot, preferred_element_type=jnp.float32
            )
        )
        grad_keys = grad_keys.at[:stop_row].add(
            ATTN_SCALE
            * jnp.einsum(
                "hgqk,qhgd->khd", grad_scores, query_block, preferred_element_type=jnp.float32
            )
        )
        grad_values = grad_values.at[:stop_row].add(
            jnp.einsum(
                "hgqk,qhgd->khd", probs_low, grad_attended, preferred_element_type=jnp.float32
            )
        )
    grad_query_rot = grad_query_parts[0].reshape(row_count, local_query, HEAD_DIM)
    grad_query_low = unrotate(grad_query_rot, cosine_lookup, sine_lookup).reshape(
        row_count, local_query * HEAD_DIM
    )
    grad_query_low = grad_query_low.astype(jnp.bfloat16)
    grad_keys_low = unrotate(grad_keys, cosine_lookup, sine_lookup).reshape(
        row_count, local_kv * HEAD_DIM
    )
    grad_keys_low = grad_keys_low.astype(jnp.bfloat16)
    grad_values_low = grad_values.reshape(row_count, local_kv * HEAD_DIM).astype(jnp.bfloat16)
    grad_query = jnp.einsum(
        "td,tc->dc", first_normed, grad_query_low, preferred_element_type=jnp.float32
    )
    grad_key = jnp.einsum(
        "td,tc->dc", first_normed, grad_keys_low, preferred_element_type=jnp.float32
    )
    grad_value = jnp.einsum(
        "td,tc->dc", first_normed, grad_values_low, preferred_element_type=jnp.float32
    )
    grad_one_part = (
        jnp.einsum("tc,dc->td", grad_query_low, query_weight, preferred_element_type=jnp.float32)
        + jnp.einsum("tc,dc->td", grad_keys_low, key_matrix, preferred_element_type=jnp.float32)
        + jnp.einsum("tc,dc->td", grad_values_low, value_matrix, preferred_element_type=jnp.float32)
    )
    grad_one = lax.psum(grad_one_part.astype(jnp.bfloat16), "tensor").astype(jnp.float32)
    grad_first_gain = jnp.sum(grad_one * unit_one, 0)
    grad_unit_one = grad_one * first_gain
    grad_tokens = grad_hidden + scale_one * (
        grad_unit_one - unit_one * jnp.mean(grad_unit_one * unit_one, -1, keepdims=True)
    )
    reduced = lax.psum(
        (
            grad_first_gain,
            grad_query,
            grad_key,
            grad_value,
            grad_output,
            grad_second_gain,
            grad_router,
            squared_local,
        ),
        "expert",
    )
    loss_value = reduced[7] / (2.0 * model_width * valid_total)
    return (
        output.astype(jnp.bfloat16),
        loss_value,
        grad_tokens,
        reduced[0],
        reduced[1],
        reduced[2],
        reduced[3],
        reduced[4],
        reduced[5],
        reduced[6],
        grad_expert_in,
        grad_expert_out,
    )


def solution(mesh):
    return jax.shard_map(
        per_device,
        mesh=mesh,
        in_specs=(
            P("expert", None),
            P("expert", None),
            P("expert"),
            P("expert", None),
            P(),
            P(None, "tensor"),
            P(None, "tensor"),
            P(None, "tensor"),
            P("tensor", None),
            P(),
            P(),
            P("expert", None, None, "tensor"),
            P("expert", "tensor", None),
        ),
        out_specs=(
            P("expert", None),
            P(),
            P("expert", None),
            P(),
            P(None, "tensor"),
            P(None, "tensor"),
            P(None, "tensor"),
            P("tensor", None),
            P(),
            P(),
            P("expert", None, None, "tensor"),
            P("expert", "tensor", None),
        ),
        check_vma=False,
    )
```

profile of v0, /device:TPU:0, one launch (start us, length us, event | category | flops | bytes accessed | tf_op | source)
XLA Modules:
  0.0 2694.3 jit_solution(5498400139283303845)
XLA Ops:
  26.2 33.0 %gather_fusion.5 = s32[4096]{0:T(1024)S(1)} fusion(s32[512,32]{0,1:T(8,128)S(1)} %bitcast_bitcast_fusion, s32[4096]{0:T(1024)S(1)} %reshape.422), kind=kCustom, calls=%fused_computation.5 | custom fusion | bytes 65536 | tf_op jit(solution)/shard_map/jit(take_along_axis)/gather | solution.py:63
  60.4 15.5 scatter_custom_fusion
  82.1 26.9 gather_fusion
  109.0 21.2 gather.23
  137.8 278.8 %all_to_all.60 = bf16[8,8,192,512]{3,2,1,0:T(8,128)(2,1)S(1)} all-to-all(bf16[8,8,192,512]{3,2,1,0:T(8,128)(2,1)S(1)} %bitcast.210), channel_id=1, replica_groups=mesh['expert'=8,'tensor'=4] {'expert'}, dimensions={0} | all-to-all | bytes 25165824 | tf_op jit(solution)/shard_map/all_to_all | solution.py:171
  421.8 12.5 fusion.83
  434.9 540.7 %collective-permute-done = f32[8,1536,2,128]{3,1,2,0:T(8,128)S(1)} collective-permute-done((f32[8,1536,2,128]{3,1,2,0:T(8,128)}, f32[8,1536,2,128]{3,1,2,0:T(8,128)S(1)}, u32[]{:S(2)}, u32[]{:S(2)}) %collective-permute-start) | collective-permute-done | bytes 12582944 | tf_op jit(solution)/shard_map/ppermute | solution.py:18
  1013.6 269.8 %all-to-all-done.1 = bf16[8,8,192,512]{3,2,0,1:T(8,128)(2,1)} async-done(((bf16[8,8,192,512]{3,2,0,1:T(8,128)(2,1)}), bf16[8,8,192,512]{3,2,0,1:T(8,128)(2,1)}, u32[]{:S(2)}, u32[]{:S(2)}) %all-to-all-start.1) | async-done | bytes 12582944 | tf_op jit(solution)/shard_map/all_to_all | solution.py:186
  1283.3 23.0 copy.103
  1313.4 27.1 %gather_fusion.1 = bf16[4096,1024]{1,0:T(8,128)(2,1)} fusion(bf16[6144,1024]{1,0:T(8,128)(2,1)} %bitcast.205, s32[4096]{0:T(1024)S(1)} %broadcast_clamp_fusion), kind=kCustom, calls=%fused_computation.1 | custom fusion | bytes 16793600 | tf_op jit(solution)/shard_map/gather | solution.py:187
  1351.7 20.1 psum.101
  1372.7 34.3 %gather_fusion.2 = f32[6144]{0:T(1024)S(1)} fusion(f32[4096]{0:T(1024)S(1)} %div.124, s32[6144]{0:T(1024)S(1)} %get-tuple-element.129), kind=kCustom, calls=%fused_computation.2 | custom fusion | bytes 73728 | tf_op jit(solution)/shard_map/gather | solution.py:200
  1410.1 26.9 gather_fusion.3
  1437.0 31.3 %reshape.381 = f32[32,192,2,512]{3,2,1,0:T(2,128)} reshape(bf16[6144,1024]{1,0:T(8,128)(2,1)} %gather_fusion.3) | data formatting | bytes 37748736 | tf_op jit(solution)/shard_map/convert_element_type | solution.py:201
  1468.2 13.5 fusion.2
  1481.8 272.4 %all_to_all.61 = bf16[8,8,192,512]{3,2,1,0:T(8,128)(2,1)S(1)} all-to-all(bf16[8,8,192,512]{3,2,1,0:T(8,128)(2,1)S(1)} %bitcast.217), channel_id=1, replica_groups=mesh['expert'=8,'tensor'=4] {'expert'}, dimensions={0} | all-to-all | bytes 25165824 | tf_op jit(solution)/shard_map/all_to_all | solution.py:202
  1764.1 269.5 %collective-permute-done.1 = f32[8,1536,128]{2,1,0:T(8,128)} collective-permute-done((f32[8,1536,128]{2,1,0:T(8,128)}, f32[8,1536,128]{2,1,0:T(8,128)}, u32[]{:S(2)}, u32[]{:S(2)}) %collective-permute-start.1) | collective-permute-done | bytes 6291488 | tf_op jit(solution)/shard_map/ppermute | solution.py:18
  2033.6 12.6 fusion.17
  2063.6 276.9 %all_to_all.62 = bf16[8,8,192,512]{3,2,0,1:T(8,128)(2,1)S(1)} all-to-all(bf16[8,8,192,512]{3,2,0,1:T(8,128)(2,1)S(1)} %copy.109), channel_id=1, replica_groups=mesh['expert'=8,'tensor'=4] {'expert'}, dimensions={1} | all-to-all | bytes 25165824 | tf_op jit(solution)/shard_map/all_to_all | solution.py:230
  2340.5 49.8 %copy.110 = bf16[32,192,2,512]{3,2,1,0:T(2,128)(2,1)S(1)} copy(bf16[32,192,2,512]{3,1,0,2:T(8,128)(2,1)S(1)} %bitcast.214) | data formatting | bytes 25165824 | tf_op jit(solution)/shard_map/transpose | solution.py:165
  2397.3 27.1 %gather_fusion.4 = bf16[4096,1024]{1,0:T(8,128)(2,1)} fusion(bf16[6144,1024]{1,0:T(8,128)(2,1)} %bitcast.204, s32[4096]{0:T(1024)S(1)} %broadcast_clamp_fusion), kind=kCustom, calls=%fused_computation.4 | custom fusion | bytes 16793600 | tf_op jit(solution)/shard_map/gather | solution.py:232
  2458.3 28.1 %all-reduce.12.cloned.1.call-done = f32[512,1024]{1,0:T(8,128)} async-done(((f32[512,1024]{1,0:T(8,128)}), f32[512,1024]{1,0:T(8,128)}) %all-reduce.12.cloned.1.call-update) | async-done | bytes 2097168 | tf_op jit(solution)/shard_map/psum | solution.py:233
  2543.1 23.5 all-reduce
  2571.1 108.7 %all-reduce.16.cloned.1.call-done = (f32[1024,256]{1,0:T(8,128)}, f32[1024,128]{1,0:T(8,128)}, f32[1024,128]{1,0:T(8,128)}, f32[256,1024]{1,0:T(8,128)}, f32[1024,32]{0,1:T(8,128)}) async-done(((f32[1024,256]{1,0:T(8,128)}, f32[1024,128]{1,0:T(8,128)}, f32[1024,128]{1,0:T(8,128)}, f32[256,1024]{1,0:T(8,128)}, f32[1024,32]{0,1:T(8,128)}), (f32[1024,256]{1,0:T(8,128)}, f32[1024,128]{1,0:T(8,128)}, ...) | async-done | bytes 3276816 | tf_op jit(solution)/shard_map/psum | solution.py:317
  (262 shorter events, 232.2 us)
Async XLA Ops:
  7.2 414.7 %copy-start = (bf16[8,2,512,128]{3,2,1,0:T(8,128)(2,1)S(1)}, bf16[8,2,512,128]{3,2,1,0:T(8,128)(2,1)}, u32[]{:S(2)}) copy-start(bf16[8,2,512,128]{3,2,1,0:T(8,128)(2,1)} %param.32) | copy-start | bytes 6291460
  7.2 71.3 %all-reduce.8.cloned.1.call-start = ((), (), s32[]{:S(2)}) async-start(), calls=%async_computation.4 | async-start | bytes 4194304 | tf_op jit(solution)/shard_map/psum | solution.py:148
  59.4 22.5 copy-start.52
  80.5 28.5 %copy-start.56 = (f32[512]{0:T(512)}, f32[512]{0:T(512)S(1)}, u32[]{:S(2)}) copy-start(f32[512]{0:T(512)S(1)} %add_rsqrt_fusion) | copy-start | bytes 6148
  82.1 930.8 %copy-start.1 = (bf16[512,1024]{1,0:T(8,128)(2,1)}, bf16[512,1024]{1,0:T(8,128)(2,1)S(1)}, u32[]{:S(2)}) copy-start(bf16[512,1024]{1,0:T(8,128)(2,1)S(1)} %multiply_convert_fusion.5) | copy-start | bytes 3145732
  434.4 541.2 %collective-permute-start = (f32[8,1536,2,128]{3,1,2,0:T(8,128)}, f32[8,1536,2,128]{3,1,2,0:T(8,128)S(1)}, u32[]{:S(2)}, u32[]{:S(2)}) collective-permute-start(f32[8,1536,2,128]{3,1,2,0:T(8,128)} %fusion.83), channel_id=1, source_target_pairs={{0,16},{4,20},{8,24},{12,28},{16,0},{20,4},{24,8},{28,12},{1,17},{... | collective-permute-start | bytes 37748744 | tf_op jit(solution)/shard_map/ppermute | solution.py:18
  1004.4 278.9 %all-to-all-start.1 = ((bf16[8,8,192,512]{3,2,0,1:T(8,128)(2,1)}), bf16[8,8,192,512]{3,2,0,1:T(8,128)(2,1)}, u32[]{:S(2)}, u32[]{:S(2)}) async-start(bf16[8,8,192,512]{3,2,0,1:T(8,128)(2,1)} %copy.102), calls=%async_computation.1 | async-start | bytes 25165824 | tf_op jit(solution)/shard_map/all_to_all | solution.py:186
  1009.9 397.1 %all-reduce.10.cloned.1.call-start = ((), (), s32[]{:S(2)}) async-start(), calls=%async_computation.5 | async-start | bytes 4194304 | tf_op jit(solution)/shard_map/psum | solution.py:191
  1013.4 293.0 %copy-start.29 = (f32[512,8]{0,1:T(8,128)}, f32[512,8]{0,1:T(8,128)S(1)}, u32[]{:S(2)}) copy-start(f32[512,8]{0,1:T(8,128)S(1)} %select_reduce_fusion.1) | copy-start | bytes 49156
  1013.4 293.0 %copy-start.50 = (f32[512]{0:T(512)}, f32[512]{0:T(512)S(1)}, u32[]{:S(2)}) copy-start(f32[512]{0:T(512)S(1)} %reduce_max.19) | copy-start | bytes 6148
  1013.4 292.9 %copy-start.54 = (f32[512]{0:T(512)}, f32[512]{0:T(512)S(1)}, u32[]{:S(2)}) copy-start(f32[512]{0:T(512)S(1)} %fusion.53) | copy-start | bytes 6148
  1350.3 1136.1 %all-reduce.12.cloned.1.call-start = ((), (), s32[]{:S(2)}) async-start(), calls=%async_computation.6 | async-start | bytes 4194304 | tf_op jit(solution)/shard_map/psum | solution.py:233
  1372.5 34.5 %copy-start.58 = (f32[512]{0:T(512)}, f32[512]{0:T(512)S(1)}, u32[]{:S(2)}) copy-start(f32[512]{0:T(512)S(1)} %convert_multiply_fusion.3) | copy-start | bytes 6148
  1410.1 26.9 copy-start.3
  1762.4 271.2 %collective-permute-start.1 = (f32[8,1536,128]{2,1,0:T(8,128)}, f32[8,1536,128]{2,1,0:T(8,128)}, u32[]{:S(2)}, u32[]{:S(2)}) collective-permute-start(f32[8,1536,128]{2,1,0:T(8,128)} %fusion.84), channel_id=1, source_target_pairs={{0,16},{4,20},{8,24},{12,28},{16,0},{20,4},{24,8},{28,12},{1,17},{... | collective-permute-start | bytes 18874376 | tf_op jit(solution)/shard_map/ppermute | solution.py:18
  2436.3 104.8 %all-reduce.14.cloned.1.call-start = ((), (), s32[]{:S(2)}) async-start(), calls=%async_computation.7 | async-start | bytes 2097152 | tf_op jit(solution)/shard_map/psum | solution.py:311
  2436.8 20.5 copy-start.39
  2436.8 20.6 copy-start.2
  2436.8 49.7 %copy-start.41 = (bf16[1024,32]{0,1:T(8,128)(2,1)S(1)}, bf16[1024,32]{0,1:T(8,128)(2,1)}, u32[]{:S(2)}) copy-start(bf16[1024,32]{0,1:T(8,128)(2,1)} %param.31) | copy-start | bytes 196612
  2436.8 49.7 %copy-start.53 = (f32[1024]{0:T(1024)S(1)}, f32[1024]{0:T(1024)}, u32[]{:S(2)}) copy-start(f32[1024]{0:T(1024)} %param.30) | copy-start | bytes 12292
  2436.8 49.6 %copy-start.57 = (f32[512]{0:T(512)S(1)}, f32[512]{0:T(512)}, u32[]{:S(2)}) copy-start(f32[512]{0:T(512)} %copy-done.56) | copy-start | bytes 6148
  2458.3 33.2 %copy-start.14 = (bf16[512,1024]{1,0:T(8,128)(2,1)S(1)}, bf16[512,1024]{1,0:T(8,128)(2,1)}, u32[]{:S(2)}) copy-start(bf16[512,1024]{1,0:T(8,128)(2,1)} %param.22) | copy-start | bytes 3145732
  2458.3 33.2 %copy-start.59 = (f32[512]{0:T(512)S(1)}, f32[512]{0:T(512)}, u32[]{:S(2)}) copy-start(f32[512]{0:T(512)} %copy-done.58) | copy-start | bytes 6148
  2504.5 175.2 %all-reduce.16.cloned.1.call-start = ((), (), s32[]{:S(2)}) async-start(), calls=%async_computation.8 | async-start | bytes 6553600 | tf_op jit(solution)/shard_map/psum | solution.py:317
  (55 other events, 273.8 us)
Sparse Core Ops, SparseCore 0:
  24.4 54.1 all-reduce.7
  1350.5 49.7 all-reduce.9
  2436.4 50.0 all-reduce.11
  2504.7 36.3 all-reduce.13
  2545.7 134.0 all-reduce.15
where the time goes:
time: 2700 us; the launch traced here: 2690 us
  waiting for transfers between devices  1230 us (46%)
  blocking collectives  883 us (33%)
  local copies, waits for them, and re-layouts  378 us (14%)
  matrix products  94.3 us (3%)
  other arithmetic  84.3 us (3%)
    ppermute x2, waiting for transfers between devices, shifted(): return lax.ppermute(value, axis, pairs)  810 us
    all_to_all x1, blocking collectives, per_device(): lax.all_to_all(send_rows, 'expert', split_axis=0, concat_axis=2, tiled=True)  279 us
    all_to_all x1, blocking collectives, per_device(): lax.all_to_all(grad_slot_rows, 'expert', split_axis=1, concat_axis=0, til...  277 us
    all_to_all x1, blocking collectives, per_device(): lax.all_to_all(slot_rows(grad_slots.astype(jnp.bfloat16)), 'expert', spli...  272 us
    all_to_all x1, waiting for transfers between devices, per_device(): lax.all_to_all(expert_result, 'expert', split_axis=1, concat_axis=0, tile...  270 us
    psum x1, waiting for transfers between devices, per_device(): lax.psum((grad_first_gain, grad_query, grad_key, grad_value, grad_output,...  109 us
    transpose x2, local copies, waits for them, and re-layouts, slot_columns(): returned.reshape(2, expert_count, capacity, width).transpose(1, 2, 0, 3)  72.8 us
  transfers between devices with their start and end apart: 8, of which 7 were waited for; matrix products, arithmetic and copies ran while one was open for 5% of the time, Pallas kernels for 0%

commit v1 on v0

--- a/solution.py
+++ b/solution.py
@@ -10,6 +10,30 @@
 ATTN_SCALE = 0.015625
 RESIDUAL = 0.22
 THETA = 10000.0
+
+
+def cut_along(x, dim, peers):
+    shape = x.shape
+    blocks = x.reshape(*shape[:dim], peers, shape[dim] // peers, *shape[dim + 1 :])
+    return jnp.moveaxis(blocks, dim, 0)
+
+
+def joined_along(parts, dim):
+    parts = jnp.moveaxis(parts, 0, dim)
+    dims = parts.shape
+    return parts.reshape(*dims[:dim], dims[dim] * dims[dim + 1], *dims[dim + 2 :])
+
+
+def exchange_directly(x, axis, split_dim, concat_dim):
+    count, index = (lax.axis_size(axis), lax.axis_index(axis))
+    parts = cut_along(x, split_dim, count)
+    out = parts
+    for step in range(1, count):
+        target, source = ((index + step) % count, (index - step) % count)
+        sent = lax.dynamic_index_in_dim(parts, target, 0)
+        other = lax.ppermute(sent, axis, [(i, (i + step) % count) for i in range(count)])
+        out = lax.dynamic_update_slice_in_dim(out, other, source, axis=0)
+    return joined_along(out, concat_dim)
 
 
 def shifted(value, axis, steps):
@@ -183,7 +207,7 @@
     expert_result = expert_result.astype(jnp.bfloat16).reshape(
         row_local, senders, capacity, half_width
     )
-    returned = lax.all_to_all(expert_result, "expert", split_axis=1, concat_axis=0, tiled=True)
+    returned = exchange_directly(expert_result, "expert", 1, 0)
     per_route = slot_columns(returned, half_width).reshape(expert_count * capacity, model_width)[
         dest_slot
     ]

time: 2700 us -> 2730 us (1.011)
  waiting for transfers between devices: 1230 us -> 1130 us
  blocking collectives: 883 us -> 956 us
  local copies, waits for them, and re-layouts: 378 us -> 419 us
    all_to_all x1 -> x0, waiting for transfers between devices: 270 us -> none  [per_device(): lax.all_to_all(expert_result, 'expert', split_axis=1, concat_axis=0, tile...]
    ppermute x0 -> x7, waiting for transfers between devices: none -> 177 us  [exchange_directly(): lax.ppermute(sent, axis, [(i, (i + step) % count) for i in range(count)])]
    psum x1, blocking collectives: 20.1 us -> 93 us  [per_device(): valid_total = lax.psum(jnp.sum(valid_mask).astype(jnp.float32), 'expert')]
  transfers between devices with their start and end apart: 8 -> 14, of which waited for: 7 -> 10; matrix products, arithmetic and copies ran while one was open for 5% -> 5% of each run, Pallas kernels for 0% -> 0%
where the time goes in v1:
time: 2730 us; the launch traced here: 2720 us
  waiting for transfers between devices  1130 us (41%)
  blocking collectives  956 us (35%)
  local copies, waits for them, and re-layouts  419 us (15%)
  matrix products  94.2 us (3%)
  other arithmetic  87.5 us (3%)
    ppermute x2, waiting for transfers between devices, shifted(): return lax.ppermute(value, axis, pairs)  810 us
    all_to_all x1, blocking collectives, per_device(): lax.all_to_all(send_rows, 'expert', split_axis=0, concat_axis=2, tiled=True)  279 us
    all_to_all x1, blocking collectives, per_device(): lax.all_to_all(grad_slot_rows, 'expert', split_axis=1, concat_axis=0, til...  277 us
    all_to_all x1, blocking collectives, per_device(): lax.all_to_all(slot_rows(grad_slots.astype(jnp.bfloat16)), 'expert', spli...  271 us
    ppermute x7, waiting for transfers between devices, exchange_directly(): lax.ppermute(sent, axis, [(i, (i + step) % count) for i in range(count)])  177 us
    psum x1, waiting for transfers between devices, per_device(): lax.psum((grad_first_gain, grad_query, grad_key, grad_value, grad_output,...  109 us
    transpose x2, local copies, waits for them, and re-layouts, slot_columns(): returned.reshape(2, expert_count, capacity, width).transpose(1, 2, 0, 3)  99.7 us
    psum x1, blocking collectives, per_device(): valid_total = lax.psum(jnp.sum(valid_mask).astype(jnp.float32), 'expert')  93 us
  transfers between devices with their start and end apart: 14, of which 10 were waited for; matrix products, arithmetic and copies ran while one was open for 5% of the time, Pallas kernels for 0%

profile of v1, /device:TPU:0, one launch (start us, length us, event | category | flops | bytes accessed | tf_op | source)
XLA Modules:
  0.0 2719.6 jit_solution(10769241638370363145)
XLA Ops:
  26.3 33.0 %gather_fusion.5 = s32[4096]{0:T(1024)S(1)} fusion(s32[512,32]{0,1:T(8,128)S(1)} %bitcast_bitcast_fusion, s32[4096]{0:T(1024)S(1)} %reshape.420), kind=kCustom, calls=%fused_computation.5 | custom fusion | bytes 65536 | tf_op jit(solution)/shard_map/jit(take_along_axis)/gather | solution.py:87
  60.5 15.5 scatter_custom_fusion
  82.1 26.7 gather_fusion
  108.9 21.3 gather.23
  137.7 279.0 %all_to_all.45 = bf16[8,8,192,512]{3,2,1,0:T(8,128)(2,1)S(1)} all-to-all(bf16[8,8,192,512]{3,2,1,0:T(8,128)(2,1)S(1)} %bitcast.227), channel_id=1, replica_groups=mesh['expert'=8,'tensor'=4] {'expert'}, dimensions={0} | all-to-all | bytes 25165824 | tf_op jit(solution)/shard_map/all_to_all | solution.py:195
  435.0 540.8 %collective-permute-done = f32[8,1536,2,128]{3,1,2,0:T(8,128)} collective-permute-done((f32[8,1536,2,128]{3,1,2,0:T(8,128)}, f32[8,1536,2,128]{3,1,2,0:T(8,128)}, u32[]{:S(2)}, u32[]{:S(2)}) %collective-permute-start) | collective-permute-done | bytes 12582944 | tf_op jit(solution)/shard_map/ppermute | solution.py:42
  1014.1 31.0 %collective-permute-done.2 = bf16[1,8,1,192,512]{4,3,1,0,2:T(8,128)(2,1)} collective-permute-done((bf16[1,8,1,192,512]{4,3,1,0,2:T(8,128)(2,1)}, bf16[1,8,1,192,512]{4,3,1,0,2:T(8,128)(2,1)}, u32[]{:S(2)}, u32[]{:S(2)}) %collective-permute-start.2) | collective-permute-done | bytes 1572896 | tf_op jit(solution)/shard_map/ppermute | solution.py:34
  1045.9 33.4 %collective-permute-done.1 = bf16[1,8,1,192,512]{4,3,1,0,2:T(8,128)(2,1)} collective-permute-done((bf16[1,8,1,192,512]{4,3,1,0,2:T(8,128)(2,1)}, bf16[1,8,1,192,512]{4,3,1,0,2:T(8,128)(2,1)}, u32[]{:S(2)}, u32[]{:S(2)}) %collective-permute-start.1) | collective-permute-done | bytes 1572896 | tf_op jit(solution)/shard_map/ppermute | solution.py:34
  1089.9 89.6 %collective-permute-done.3 = bf16[1,8,1,192,512]{4,3,1,0,2:T(8,128)(2,1)} collective-permute-done((bf16[1,8,1,192,512]{4,3,1,0,2:T(8,128)(2,1)}, bf16[1,8,1,192,512]{4,3,1,0,2:T(8,128)(2,1)}, u32[]{:S(2)}, u32[]{:S(2)}) %collective-permute-start.3) | collective-permute-done | bytes 1572896 | tf_op jit(solution)/shard_map/ppermute | solution.py:34
  1185.8 22.9 collective-permute-done.7
  1210.3 49.9 %copy.103 = bf16[32,192,2,512]{3,2,1,0:T(2,128)(2,1)S(1)} copy(bf16[32,192,2,512]{3,1,0,2:T(8,128)(2,1)S(1)} %bitcast.226) | data formatting | bytes 25165824 | tf_op jit(solution)/shard_map/transpose | solution.py:189
  1267.2 27.0 gather_fusion.1
  1306.0 93.0 %psum.101 = f32[]{:T(128)} all-reduce(f32[]{:T(128)S(6)} %convert_element_type.123), channel_id=1, replica_groups=mesh['expert'=8,'tensor'=4] {'expert'}, use_global_device_ids=true, to_apply=%region_18.19 | all-reduce | flops 1 | bytes 8 | tf_op jit(solution)/shard_map/psum | solution.py:128
  1399.9 34.3 %gather_fusion.2 = f32[6144]{0:T(1024)S(1)} fusion(f32[4096]{0:T(1024)S(1)} %div.124, s32[6144]{0:T(1024)S(1)} %get-tuple-element.136), kind=kCustom, calls=%fused_computation.2 | custom fusion | bytes 73728 | tf_op jit(solution)/shard_map/gather | solution.py:224
  1437.3 26.8 gather_fusion.3
  1464.1 31.3 %reshape.379 = f32[32,192,2,512]{3,2,1,0:T(2,128)} reshape(bf16[6144,1024]{1,0:T(8,128)(2,1)} %gather_fusion.3) | data formatting | bytes 37748736 | tf_op jit(solution)/shard_map/convert_element_type | solution.py:225
  1508.9 271.5 %all_to_all.46 = bf16[8,8,192,512]{3,2,1,0:T(8,128)(2,1)S(1)} all-to-all(bf16[8,8,192,512]{3,2,1,0:T(8,128)(2,1)S(1)} %bitcast.233), channel_id=1, replica_groups=mesh['expert'=8,'tensor'=4] {'expert'}, dimensions={0} | all-to-all | bytes 25165824 | tf_op jit(solution)/shard_map/all_to_all | solution.py:226
  1789.8 269.6 %collective-permute-done.8 = f32[8,1536,128]{2,1,0:T(8,128)} collective-permute-done((f32[8,1536,128]{2,1,0:T(8,128)}, f32[8,1536,128]{2,1,0:T(8,128)}, u32[]{:S(2)}, u32[]{:S(2)}) %collective-permute-start.8) | collective-permute-done | bytes 6291488 | tf_op jit(solution)/shard_map/ppermute | solution.py:42
  2089.4 276.9 %all_to_all.47 = bf16[8,8,192,512]{3,2,0,1:T(8,128)(2,1)S(1)} all-to-all(bf16[8,8,192,512]{3,2,0,1:T(8,128)(2,1)S(1)} %copy.109), channel_id=1, replica_groups=mesh['expert'=8,'tensor'=4] {'expert'}, dimensions={1} | all-to-all | bytes 25165824 | tf_op jit(solution)/shard_map/all_to_all | solution.py:254
  2366.3 49.8 %copy.110 = bf16[32,192,2,512]{3,2,1,0:T(2,128)(2,1)S(1)} copy(bf16[32,192,2,512]{3,1,0,2:T(8,128)(2,1)S(1)} %bitcast.231) | data formatting | bytes 25165824 | tf_op jit(solution)/shard_map/transpose | solution.py:189
  2423.1 27.0 gather_fusion.4
  2483.7 29.0 %all-reduce.12.cloned.1.call-done = f32[512,1024]{1,0:T(8,128)} async-done(((f32[512,1024]{1,0:T(8,128)}), f32[512,1024]{1,0:T(8,128)}) %all-reduce.12.cloned.1.call-update) | async-done | bytes 2097168 | tf_op jit(solution)/shard_map/psum | solution.py:257
  2569.4 23.5 all-reduce
  2597.3 108.7 %all-reduce.16.cloned.1.call-done = (f32[1024,256]{1,0:T(8,128)}, f32[1024,128]{1,0:T(8,128)}, f32[1024,128]{1,0:T(8,128)}, f32[256,1024]{1,0:T(8,128)}, f32[1024,32]{0,1:T(8,128)}) async-done(((f32[1024,256]{1,0:T(8,128)}, f32[1024,128]{1,0:T(8,128)}, f32[1024,128]{1,0:T(8,128)}, f32[256,1024]{1,0:T(8,128)}, f32[1024,32]{0,1:T(8,128)}), (f32[1024,256]{1,0:T(8,128)}, f32[1024,128]{1,0:T(8,128)}, ...) | async-done | bytes 3276816 | tf_op jit(solution)/shard_map/psum | solution.py:341
  (288 shorter events, 289.0 us)
Async XLA Ops:
  7.2 414.7 %copy-start = (bf16[8,2,512,128]{3,2,1,0:T(8,128)(2,1)S(1)}, bf16[8,2,512,128]{3,2,1,0:T(8,128)(2,1)}, u32[]{:S(2)}) copy-start(bf16[8,2,512,128]{3,2,1,0:T(8,128)(2,1)} %param.32) | copy-start | bytes 6291460
  7.2 71.3 %all-reduce.8.cloned.1.call-start = ((), (), s32[]{:S(2)}) async-start(), calls=%async_computation.3 | async-start | bytes 4194304 | tf_op jit(solution)/shard_map/psum | solution.py:172
  24.3 1410.0 %all-reduce.10.cloned.1.call-start = ((), (), s32[]{:S(2)}) async-start(), calls=%async_computation.4 | async-start | bytes 4194304 | tf_op jit(solution)/shard_map/psum | solution.py:215
  76.2 54.0 %copy-start.51 = (pred[32,192]{1,0:T(8,128)(4,1)}, pred[32,192]{1,0:T(8,128)(4,1)S(1)}, u32[]{:S(2)}) copy-start(pred[32,192]{1,0:T(8,128)(4,1)S(1)} %broadcast_in_dim.71) | copy-start | bytes 18436
  82.1 997.5 %copy-start.1 = (bf16[512,1024]{1,0:T(8,128)(2,1)}, bf16[512,1024]{1,0:T(8,128)(2,1)S(1)}, u32[]{:S(2)}) copy-start(bf16[512,1024]{1,0:T(8,128)(2,1)S(1)} %multiply_convert_fusion.5) | copy-start | bytes 3145732
  434.4 541.3 %collective-permute-start = (f32[8,1536,2,128]{3,1,2,0:T(8,128)}, f32[8,1536,2,128]{3,1,2,0:T(8,128)}, u32[]{:S(2)}, u32[]{:S(2)}) collective-permute-start(f32[8,1536,2,128]{3,1,2,0:T(8,128)} %fusion.83), channel_id=1, source_target_pairs={{0,16},{4,20},{8,24},{12,28},{16,0},{20,4},{24,8},{28,12},{1,17},{... | collective-permute-start | bytes 37748744 | tf_op jit(solution)/shard_map/ppermute | solution.py:42
  997.2 82.4 %copy-start.41 = (bf16[1024,32]{0,1:T(8,128)(2,1)S(1)}, bf16[1024,32]{0,1:T(8,128)(2,1)}, u32[]{:S(2)}) copy-start(bf16[1024,32]{0,1:T(8,128)(2,1)} %param.31) | copy-start | bytes 196612
  1005.7 39.5 %collective-permute-start.2 = (bf16[1,8,1,192,512]{4,3,1,0,2:T(8,128)(2,1)}, bf16[1,8,1,192,512]{4,3,1,0,2:T(8,128)(2,1)}, u32[]{:S(2)}, u32[]{:S(2)}) collective-permute-start(bf16[1,8,1,192,512]{4,3,1,0,2:T(8,128)(2,1)} %get-tuple-element.124), channel_id=1, source_target_pairs={{0,8},{4,12},{8,16},{12,20},{16,24},{20,28},{24,0},{28,4},{1,9},{5... | collective-permute-start | bytes 4718600 | tf_op jit(solution)/shard_map/ppermute | solution.py:34
  1005.7 73.6 %collective-permute-start.1 = (bf16[1,8,1,192,512]{4,3,1,0,2:T(8,128)(2,1)}, bf16[1,8,1,192,512]{4,3,1,0,2:T(8,128)(2,1)}, u32[]{:S(2)}, u32[]{:S(2)}) collective-permute-start(bf16[1,8,1,192,512]{4,3,1,0,2:T(8,128)(2,1)} %get-tuple-element.125), channel_id=1, source_target_pairs={{0,4},{4,8},{8,12},{12,16},{16,20},{20,24},{24,28},{28,0},{1,5},{5... | collective-permute-start | bytes 4718600 | tf_op jit(solution)/shard_map/ppermute | solution.py:34
  1006.6 172.8 %collective-permute-start.3 = (bf16[1,8,1,192,512]{4,3,1,0,2:T(8,128)(2,1)}, bf16[1,8,1,192,512]{4,3,1,0,2:T(8,128)(2,1)}, u32[]{:S(2)}, u32[]{:S(2)}) collective-permute-start(bf16[1,8,1,192,512]{4,3,1,0,2:T(8,128)(2,1)} %get-tuple-element.123), channel_id=1, source_target_pairs={{0,12},{4,16},{8,20},{12,24},{16,28},{20,0},{24,4},{28,8},{1,13},{... | collective-permute-start | bytes 4718600 | tf_op jit(solution)/shard_map/ppermute | solution.py:34
  1009.5 171.5 %collective-permute-start.4 = (bf16[1,8,1,192,512]{4,3,1,0,2:T(8,128)(2,1)}, bf16[1,8,1,192,512]{4,3,1,0,2:T(8,128)(2,1)}, u32[]{:S(2)}, u32[]{:S(2)}) collective-permute-start(bf16[1,8,1,192,512]{4,3,1,0,2:T(8,128)(2,1)} %get-tuple-element.122), channel_id=1, source_target_pairs={{0,16},{4,20},{8,24},{12,28},{16,0},{20,4},{24,8},{28,12},{1,17},{... | collective-permute-start | bytes 4718600 | tf_op jit(solution)/shard_map/ppermute | solution.py:34
  1011.0 171.7 %collective-permute-start.5 = (bf16[1,8,1,192,512]{4,3,1,0,2:T(8,128)(2,1)}, bf16[1,8,1,192,512]{4,3,1,0,2:T(8,128)(2,1)}, u32[]{:S(2)}, u32[]{:S(2)}) collective-permute-start(bf16[1,8,1,192,512]{4,3,1,0,2:T(8,128)(2,1)} %get-tuple-element.121), channel_id=1, source_target_pairs={{0,20},{4,24},{8,28},{12,0},{16,4},{20,8},{24,12},{28,16},{1,21},{... | collective-permute-start | bytes 4718600 | tf_op jit(solution)/shard_map/ppermute | solution.py:34
  1045.1 139.1 %collective-permute-start.6 = (bf16[1,8,1,192,512]{4,3,1,0,2:T(8,128)(2,1)}, bf16[1,8,1,192,512]{4,3,1,0,2:T(8,128)(2,1)}, u32[]{:S(2)}, u32[]{:S(2)}) collective-permute-start(bf16[1,8,1,192,512]{4,3,1,0,2:T(8,128)(2,1)} %get-tuple-element.120), channel_id=1, source_target_pairs={{0,24},{4,28},{8,0},{12,4},{16,8},{20,12},{24,16},{28,20},{1,25},{... | collective-permute-start | bytes 4718600 | tf_op jit(solution)/shard_map/ppermute | solution.py:34
  1079.3 129.4 %collective-permute-start.7 = (bf16[1,8,1,192,512]{4,3,1,0,2:T(8,128)(2,1)}, bf16[1,8,1,192,512]{4,3,1,0,2:T(8,128)(2,1)}, u32[]{:S(2)}, u32[]{:S(2)}) collective-permute-start(bf16[1,8,1,192,512]{4,3,1,0,2:T(8,128)(2,1)} %get-tuple-element.119), channel_id=1, source_target_pairs={{0,28},{4,0},{8,4},{12,8},{16,12},{20,16},{24,20},{28,24},{1,29},{... | collective-permute-start | bytes 4718600 | tf_op jit(solution)/shard_map/ppermute | solution.py:34
  1304.1 1208.5 %all-reduce.12.cloned.1.call-start = ((), (), s32[]{:S(2)}) async-start(), calls=%async_computation.5 | async-start | bytes 4194304 | tf_op jit(solution)/shard_map/psum | solution.py:257
  1399.8 34.5 %copy-start.61 = (f32[512]{0:T(512)}, f32[512]{0:T(512)S(1)}, u32[]{:S(2)}) copy-start(f32[512]{0:T(512)S(1)} %convert_multiply_fusion.3) | copy-start | bytes 6148
  1788.7 270.7 %collective-permute-start.8 = (f32[8,1536,128]{2,1,0:T(8,128)}, f32[8,1536,128]{2,1,0:T(8,128)}, u32[]{:S(2)}, u32[]{:S(2)}) collective-permute-start(f32[8,1536,128]{2,1,0:T(8,128)} %fusion.84), channel_id=1, source_target_pairs={{0,16},{4,20},{8,24},{12,28},{16,0},{20,4},{24,8},{28,12},{1,17},{... | collective-permute-start | bytes 18874376 | tf_op jit(solution)/shard_map/ppermute | solution.py:42
  2462.0 105.3 %all-reduce.14.cloned.1.call-start = ((), (), s32[]{:S(2)}) async-start(), calls=%async_computation.6 | async-start | bytes 2097152 | tf_op jit(solution)/shard_map/psum | solution.py:335
  2462.3 50.3 %copy-start.42 = (bf16[1024,32]{0,1:T(8,128)(2,1)S(1)}, bf16[1024,32]{0,1:T(8,128)(2,1)}, u32[]{:S(2)}) copy-start(bf16[1024,32]{0,1:T(8,128)(2,1)} %param.31) | copy-start | bytes 196612
  2462.3 50.3 %copy-start.56 = (f32[1024]{0:T(1024)S(1)}, f32[1024]{0:T(1024)}, u32[]{:S(2)}) copy-start(f32[1024]{0:T(1024)} %param.30) | copy-start | bytes 12292
  2462.3 50.3 %copy-start.60 = (f32[512]{0:T(512)S(1)}, f32[512]{0:T(512)}, u32[]{:S(2)}) copy-start(f32[512]{0:T(512)} %copy-done.59) | copy-start | bytes 6148
  2483.7 34.0 %copy-start.14 = (bf16[512,1024]{1,0:T(8,128)(2,1)S(1)}, bf16[512,1024]{1,0:T(8,128)(2,1)}, u32[]{:S(2)}) copy-start(bf16[512,1024]{1,0:T(8,128)(2,1)} %param.22) | copy-start | bytes 3145732
  2483.7 34.0 %copy-start.62 = (f32[512]{0:T(512)S(1)}, f32[512]{0:T(512)}, u32[]{:S(2)}) copy-start(f32[512]{0:T(512)} %copy-done.61) | copy-start | bytes 6148
  2530.8 175.2 %all-reduce.16.cloned.1.call-start = ((), (), s32[]{:S(2)}) async-start(), calls=%async_computation.7 | async-start | bytes 6553600 | tf_op jit(solution)/shard_map/psum | solution.py:341
  (64 other events, 388.3 us)
Sparse Core Ops, SparseCore 0:
  24.4 54.0 all-reduce.7
  1304.2 123.0 all-reduce.9
  2462.1 50.4 all-reduce.11
  2530.9 36.3 all-reduce.13
  2572.0 134.0 all-reduce.15
